TPU v7x, 128 devices: a whole 4x4x4 slice. The times are simulated.
128 devices in a mesh: row: 8 (over x_hi, z), rep: 16 (over x_lo, y, core).
Axes of the slice: x: 4 (x_hi: 2, x_lo: 2; x = x_hi * 2 + x_lo), y: 4, z: 4, core: 2. Of those that a mesh axis runs over, the one named last changes fastest.
Arguments:
- features: bfloat16 [32768, 256], P('row'), may hold values from 0 to 2
- self_weight: bfloat16 [256, 256], replicated, may hold values from -0.375 to 0.375
- neigh_weight: bfloat16 [256, 256], replicated, may hold values from -0.375 to 0.375
- out_bias: float32 [256], replicated, may hold values from -4 to 4
- tile_masks: int32 [32768, 128, 128], P('row', 'rep'), may hold values 0 or 1
- tile_live: int32 [256, 128], P('row', 'rep'), may hold values from 0 to 1, as said below
- tile_columns: int32 [256, 128], P('row', 'rep'), may hold values from 0 to 1
- node_degree: int32 [32768], P(('row', 'rep')), may hold values from 128 to 511
- cotangent: bfloat16 [32768, 256], P(('row', 'rep')), may hold values from -6 to 6
Outputs:
- hidden_out: bfloat16 [32768, 256], P(('row', 'rep'))
- grad_features: bfloat16 [32768, 256], P(('row', 'rep'))
- grad_self: float32 [256, 256], replicated
- grad_neigh: float32 [256, 256], replicated
- grad_bias: float32 [256], replicated
Inputs may be any that keep to these rules, and one draw needn't show every extreme that they name: `tile_masks`: an edge bit; bits of slots without a tile are not read. `tile_live`: 1 where the slot holds a tile. `tile_columns`: the covered block among the 2 blocks of that column set and panel.
All inputs are finite; a program needn't handle non-finite values. No bound on the sum of `tile_masks` on one device may be relied on, other than what follows from the above.
Results may differ from a plain program's by a relative error of at most 0.0053.
Values may be sent and summed in bfloat16 or wider, within the bound.
A program may use at most 128 MiB of HBM per device.

v0:
```python
import math
import jax
import jax.numpy as jnp
from jax import lax
from jax.sharding import PartitionSpec as P


def activation(values):
    return jax.nn.gelu(values, approximate=True)


def per_device(
    features,
    self_weight,
    neigh_weight,
    out_bias,
    tile_masks,
    tile_live,
    tile_columns,
    node_degree,
    cotangent,
):
    row_devices = lax.axis_size("row")
    rep_devices = lax.axis_size("rep")
    panel_rows, width = features.shape
    share_rows = node_degree.shape[0]
    panel_count = tile_masks.shape[1]
    tile_size = tile_masks.shape[2]
    block_rows = panel_rows // tile_size
    set_blocks = share_rows // tile_size
    column_rows = panel_count * share_rows
    contract_first = (((0,), (0,)), ((), ()))
    contract_second = (((1,), (1,)), ((), ()))
    block_ids = jnp.arange(set_blocks, dtype=jnp.int32)
    selected = (tile_columns[:, :, None] == block_ids[None, None, :]) & (tile_live[:, :, None] != 0)
    keeper = selected.astype(jnp.bfloat16)
    dense = tile_masks.reshape(block_rows, tile_size, panel_count, 1, tile_size).astype(
        jnp.bfloat16
    )
    dense = (dense * keeper[:, None, :, :, None]).reshape(panel_rows, column_rows)
    own = lax.dynamic_slice_in_dim(features, lax.axis_index("rep") * share_rows, share_rows, 0)
    strip = dense
    partial_sums = jnp.dot(
        strip, lax.all_gather(own, "row", axis=0, tiled=True), preferred_element_type=jnp.float32
    )
    agg_sum = lax.psum_scatter(partial_sums, "rep", scatter_dimension=0, tiled=True)
    degree = node_degree.astype(jnp.float32)[:, None]
    mean = (agg_sum / degree).astype(jnp.bfloat16)
    pre = (
        jnp.dot(own, self_weight, preferred_element_type=jnp.float32)
        + jnp.dot(mean, neigh_weight, preferred_element_type=jnp.float32)
        + out_bias
    )
    result, pull = jax.vjp(activation, pre)
    hidden_out = result.astype(jnp.bfloat16)
    dpre = pull(cotangent.astype(jnp.float32))[0]
    dpre_b = dpre.astype(jnp.bfloat16)
    scale = 1.0 / math.sqrt(share_rows * row_devices * rep_devices)
    self_term = (
        lax.dot_general(own, dpre_b, contract_first, preferred_element_type=jnp.float32) * scale
    )
    neigh_term = (
        lax.dot_general(mean, dpre_b, contract_first, preferred_element_type=jnp.float32) * scale
    )
    bias_term = jnp.sum(dpre, axis=0) * scale
    grad_self, grad_neigh, grad_bias = lax.psum((self_term, neigh_term, bias_term), ("row", "rep"))
    message = (
        lax.dot_general(dpre_b, neigh_weight, contract_second, preferred_element_type=jnp.float32)
        / degree
    ).astype(jnp.bfloat16)
    direct = lax.dot_general(
        dpre_b, self_weight, contract_second, preferred_element_type=jnp.float32
    )
    strip = dense
    partial_back = lax.dot_general(
        strip,
        lax.all_gather(message, "rep", axis=0, tiled=True),
        contract_first,
        preferred_element_type=jnp.float32,
    )
    spread = lax.psum_scatter(
        partial_back.astype(jnp.bfloat16), "row", scatter_dimension=0, tiled=True
    ).astype(jnp.float32)
    grad_features = (direct + spread).astype(jnp.bfloat16)
    return (hidden_out, grad_features, grad_self, grad_neigh, grad_bias)


def solution(mesh):
    return jax.shard_map(
        per_device,
        mesh=mesh,
        in_specs=(
            P("row", None),
            P(),
            P(),
            P(),
            P("row", "rep", None),
            P("row", "rep"),
            P("row", "rep"),
            P(("row", "rep")),
            P(("row", "rep"), None),
        ),
        out_specs=(P(("row", "rep"), None), P(("row", "rep"), None), P(), P(), P()),
        check_vma=False,
    )
```

profile of v0, /device:TPU:1, one launch (start us, length us, event | category | flops | bytes accessed | tf_op | source)
XLA Modules:
  0.0 428.5 jit_solution(4350122207436884132)
XLA Ops:
  7.2 0.0 copy-start
  7.2 0.0 all-gather.3.cloned.1.call-start
  7.2 1.5 copy-done
  8.8 0.7 constant_dynamic-slice_fusion
  9.4 0.0 all-gather.3.cloned.1.call-update
  9.5 0.0 reduce-scatter.3.cloned.1.call-start
  9.5 0.8 copy.14
  10.3 0.7 broadcast_compare_fusion
  11.0 0.1 copy.15
  11.1 6.3 %convert_element_type.45 = bf16[4096,8,128]{2,1,0:T(8,128)(2,1)S(1)} convert(s32[4096,8,128]{2,1,0:T(8,128)} %param.13) | non-fusion elementwise | flops 4194304 | bytes 25165824 | tf_op jit(solution)/shard_map/convert_element_type | solution.py:37
  17.4 0.1 fusion.13
  17.5 19.8 %broadcast_multiply_fusion = bf16[32,128,8,2,128]{4,3,2,1,0:T(2,128)(2,1)} fusion(bf16[32,8,2]{2,1,0:T(8,128)(2,1)S(1)} %fusion.13, bf16[32,128,8,128]{3,2,1,0:T(8,128)(2,1)S(1)} %bitcast.15), kind=kLoop, calls=%fused_computation | loop fusion | flops 8388608 | bytes 25166848 | tf_op jit(solution)/shard_map/mul | solution.py:40
  37.3 27.8 %mul.80 = bf16[4096,2048]{1,0:T(8,128)(2,1)} reshape(bf16[32,128,8,2,128]{4,3,2,1,0:T(2,128)(2,1)} %broadcast_multiply_fusion) | data formatting | bytes 33554432 | tf_op jit(solution)/shard_map/mul | solution.py:40
  65.1 0.0 copy-start.4
  65.1 0.0 copy-start.2
  65.1 0.0 copy-start.3
  65.1 0.0 copy-start.6
  65.1 0.0 copy-start.7
  65.1 0.0 copy-start.8
  65.1 0.0 all-gather.3.cloned.1.call-done
  65.2 12.6 %fusion.17 = f32[4096,256]{1,0:T(8,128)} fusion(bf16[4096,2048]{1,0:T(8,128)(2,1)} %mul.80, bf16[2048,256]{1,0:T(8,128)(2,1)} %all-gather.3.cloned.1.call-done), kind=kOutput, calls=%fused_computation.33 | convolution fusion | flops 4294967296 | bytes 22020096 | tf_op jit(solution)/shard_map/dot_general | solution.py:43
  77.8 0.0 reduce-scatter.3.cloned.1.call-update
  77.8 0.0 all-gather.5.cloned.1.call-start
  77.8 0.0 copy-done.4
  77.9 0.0 copy-done.2
  77.9 0.0 copy-done.3
  77.9 0.2 fusion.16
  78.1 66.0 %reduce-scatter.3.cloned.1.call-done = f32[256,256]{1,0:T(8,128)} async-done(((f32[4096,256]{1,0:T(8,128)}), f32[256,256]{1,0:T(8,128)}) %reduce-scatter.3.cloned.1.call-update) | async-done | bytes 262160 | tf_op jit(solution)/shard_map/reduce_scatter | solution.py:46
  144.1 0.0 copy-done.6
  144.1 0.0 copy-done.7
  144.1 0.0 copy-done.8
  144.1 2.0 fusion.14
  146.1 0.9 fusion.2
  147.0 0.0 all-gather.5.cloned.1.call-update
  147.0 0.0 copy-start.5
  147.0 0.0 copy-start.1
  147.0 0.2 reduce-scatter.5.cloned.1.call-start
  147.3 36.9 %all-gather.5.cloned.1.call-done = bf16[4096,256]{1,0:T(8,128)(2,1)} async-done(((bf16[256,256]{1,0:T(8,128)(2,1)}), bf16[4096,256]{1,0:T(8,128)(2,1)}) %all-gather.5.cloned.1.call-update) | async-done | bytes 2097168 | tf_op jit(solution)/shard_map/all_gather | solution.py:77
  184.1 12.3 %convolution_convert_fusion = bf16[2048,256]{1,0:T(8,128)(2,1)} fusion(bf16[4096,2048]{1,0:T(8,128)(2,1)} %mul.80, bf16[4096,256]{1,0:T(8,128)(2,1)} %all-gather.5.cloned.1.call-done), kind=kOutput, calls=%fused_computation.1 | convolution fusion | flops 4295491584 | bytes 19922944 | tf_op jit(solution)/shard_map/dot_general | solution.py:75
  196.4 0.0 reduce-scatter.5.cloned.1.call-update
  196.4 0.0 all-reduce.3.cloned.1.call-start
  196.5 0.9 convolution_multiply_fusion.1
  197.4 0.0 copy-done.5
  197.4 1.0 convolution_multiply_fusion
  198.4 0.0 all-reduce.3.cloned.1.call-update
  198.5 66.0 %psum.23 = f32[256]{0:T(256)} all-reduce(f32[256]{0:T(256)S(1)} %broadcast_multiply_fusion.1), channel_id=1, replica_groups=mesh['row'=8,'rep'=16] {'row','rep'}, use_global_device_ids=true, to_apply=%region_5.0 | all-reduce | flops 256 | bytes 2048 | tf_op jit(solution)/shard_map/psum | solution.py:66
  264.4 1.8 reduce-scatter.5.cloned.1.call-done
  266.2 1.8 fusion.1
  268.0 150.7 %all-reduce.3.cloned.1.call-done = (f32[256,256]{1,0:T(8,128)}, f32[256,256]{1,0:T(8,128)}) async-done(((f32[256,256]{1,0:T(8,128)}, f32[256,256]{1,0:T(8,128)}), (f32[256,256]{1,0:T(8,128)}, f32[256,256]{1,0:T(8,128)})) %all-reduce.3.cloned.1.call-update) | async-done | bytes 524304 | tf_op jit(solution)/shard_map/psum | solution.py:66
  418.6 1.7 copy.18
  420.3 1.7 copy.19
  422.0 0.0 copy-done.1
  (2 shorter events, 0.0 us)
Async XLA Ops:
  7.2 1.6 copy-start
  7.2 58.0 %all-gather.3.cloned.1.call-start = ((), (), s32[]{:S(2)}) async-start(), calls=%async_computation.2 | async-start | bytes 1179648 | tf_op jit(solution)/shard_map/all_gather | solution.py:44
  9.5 134.6 %reduce-scatter.3.cloned.1.call-start = ((), (), s32[]{:S(2)}) async-start(), calls=%async_computation.3 | async-start | bytes 4456448 | tf_op jit(solution)/shard_map/reduce_scatter | solution.py:46
  65.1 12.7 %copy-start.4 = (s32[256]{0:T(256)S(1)}, s32[256]{0:T(256)}, u32[]{:S(2)}) copy-start(s32[256]{0:T(256)} %param.16) | copy-start | bytes 3076
  65.1 12.8 %copy-start.2 = (bf16[256,256]{1,0:T(8,128)(2,1)S(1)}, bf16[256,256]{1,0:T(8,128)(2,1)}, u32[]{:S(2)}) copy-start(bf16[256,256]{1,0:T(8,128)(2,1)} %constant_dynamic-slice_fusion) | copy-start | bytes 393220
  65.1 12.8 %copy-start.3 = (bf16[256,256]{1,0:T(8,128)(2,1)S(1)}, bf16[256,256]{1,0:T(8,128)(2,1)}, u32[]{:S(2)}) copy-start(bf16[256,256]{1,0:T(8,128)(2,1)} %param.10) | copy-start | bytes 393220
  65.1 79.0 %copy-start.6 = (bf16[256,256]{1,0:T(8,128)(2,1)S(1)}, bf16[256,256]{1,0:T(8,128)(2,1)}, u32[]{:S(2)}) copy-start(bf16[256,256]{1,0:T(8,128)(2,1)} %param.17) | copy-start | bytes 393220
  65.1 78.9 %copy-start.7 = (bf16[256,256]{1,0:T(8,128)(2,1)S(1)}, bf16[256,256]{1,0:T(8,128)(2,1)}, u32[]{:S(2)}) copy-start(bf16[256,256]{1,0:T(8,128)(2,1)} %param.11) | copy-start | bytes 393220
  65.1 78.9 %copy-start.8 = (f32[256]{0:T(256)S(1)}, f32[256]{0:T(256)}, u32[]{:S(2)}) copy-start(f32[256]{0:T(256)} %param.12) | copy-start | bytes 3076
  77.8 106.3 %all-gather.5.cloned.1.call-start = ((), (), s32[]{:S(2)}) async-start(), calls=%async_computation.4 | async-start | bytes 2228224 | tf_op jit(solution)/shard_map/all_gather | solution.py:77
  147.0 50.4 %copy-start.5 = (f32[256,256]{1,0:T(8,128)S(1)}, f32[256,256]{1,0:T(8,128)}, u32[]{:S(2)}) copy-start(f32[256,256]{1,0:T(8,128)} %reduce-scatter.3.cloned.1.call-done) | copy-start | bytes 786436
  147.0 274.9 %copy-start.1 = (bf16[4096,256]{1,0:T(8,128)(2,1)S(1)}, bf16[4096,256]{1,0:T(8,128)(2,1)}, u32[]{:S(2)}) copy-start(bf16[4096,256]{1,0:T(8,128)(2,1)} %param.9) | copy-start | bytes 6291460
  147.0 119.2 %reduce-scatter.5.cloned.1.call-start = ((), (), s32[]{:S(2)}) async-start(), calls=%async_computation.5 | async-start | bytes 1179648 | tf_op jit(solution)/shard_map/reduce_scatter | solution.py:81
  196.4 222.2 %all-reduce.3.cloned.1.call-start = ((), (), s32[]{:S(2)}) async-start(), calls=%async_computation.6 | async-start | bytes 1048576 | tf_op jit(solution)/shard_map/psum | solution.py:66
Sparse Core Ops, SparseCore 0:
  11.0 48.4 all-gather.2
  77.9 66.0 reduce-scatter.2
  147.1 36.9 all-gather.4
  196.6 69.5 reduce-scatter.4
  272.3 146.2 all-reduce.2
where the time goes:
time: 430 us; the launch traced here: 429 us
  waiting for transfers between devices  255 us (59%)
  blocking collectives  66 us (15%)
  local copies, waits for them, and re-layouts  34.2 us (8%)
  matrix products  31.7 us (7%)
  other arithmetic  27 us (6%)
  between operations  13.9 us (3%)
    psum x1, waiting for transfers between devices, per_device(): lax.psum((self_term, neigh_term, bias_term), ('row', 'rep'))  151 us
    reduce_scatter x1, waiting for transfers between devices, per_device(): lax.psum_scatter(partial_sums, 'rep', scatter_dimension=0, tiled=True)  66 us
    psum x1, blocking collectives, per_device(): lax.psum((self_term, neigh_term, bias_term), ('row', 'rep'))  66 us
    all_gather x1, waiting for transfers between devices, per_device(): lax.all_gather(message, 'rep', axis=0, tiled=True)  36.9 us
    mul x1, local copies, waits for them, and re-layouts, per_device(): dense * keeper[:, None, :, :, None]  27.8 us
    mul x1, other arithmetic, per_device(): dense * keeper[:, None, :, :, None]  19.8 us
    dot_general x1, matrix products, per_device(): jnp.dot(strip, lax.all_gather(own, 'row', axis=0, tiled=True), preferred_...  12.6 us
    dot_general x1, matrix products, per_device(): lax.dot_general(strip, lax.all_gather(message, 'rep', axis=0, tiled=True)...  12.3 us
  transfers between devices with their start and end apart: 5, of which 4 were waited for; matrix products, arithmetic and copies ran while one was open for 14% of the time, Pallas kernels for 0%

commit v1 on v0

--- a/solution.py
+++ b/solution.py
@@ -20,6 +20,14 @@
     node_degree,
     cotangent,
 ):
+
+    def _manage_run(own_rows):
+        axis_key = "row"
+        dev_axis = "rep"
+        for w in (axis_key, dev_axis):
+            own_rows = lax.psum(own_rows, axis_name=w)
+        return own_rows
+
     row_devices = lax.axis_size("row")
     rep_devices = lax.axis_size("rep")
     panel_rows, width = features.shape
@@ -63,7 +71,7 @@
         lax.dot_general(mean, dpre_b, contract_first, preferred_element_type=jnp.float32) * scale
     )
     bias_term = jnp.sum(dpre, axis=0) * scale
-    grad_self, grad_neigh, grad_bias = lax.psum((self_term, neigh_term, bias_term), ("row", "rep"))
+    grad_self, grad_neigh, grad_bias = _manage_run((self_term, neigh_term, bias_term))
     message = (
         lax.dot_general(dpre_b, neigh_weight, contract_second, preferred_element_type=jnp.float32)
         / degree

time: 430 us -> 476 us (1.11)
  waiting for transfers between devices: 255 us -> 313 us
  blocking collectives: 66 us -> 53.8 us
    psum x1 -> x2, waiting for transfers between devices: 151 us -> 190 us  [_manage_run(): own_rows = lax.psum(own_rows, axis_name=w)]
    reduce_scatter x1, waiting for transfers between devices: 1.76 us -> 23.4 us  [per_device(): lax.psum_scatter(partial_back.astype(jnp.bfloat16), 'row', scatter_dimens...]
    psum x1 -> x2, blocking collectives: 66 us -> 53.8 us  [_manage_run(): own_rows = lax.psum(own_rows, axis_name=w)]
  transfers between devices with their start and end apart: 5 -> 6, of which waited for: 4 -> 5; matrix products, arithmetic and copies ran while one was open for 14% -> 15% of each run, Pallas kernels for 0% -> 0%
where the time goes in v1:
time: 476 us; the launch traced here: 475 us
  waiting for transfers between devices  313 us (66%)
  blocking collectives  53.8 us (11%)
  local copies, waits for them, and re-layouts  34.2 us (7%)
  matrix products  32.7 us (7%)
  other arithmetic  27 us (6%)
  between operations  14.2 us (3%)
    psum x2, waiting for transfers between devices, _manage_run(): own_rows = lax.psum(own_rows, axis_name=w)  190 us
    reduce_scatter x1, waiting for transfers between devices, per_device(): lax.psum_scatter(partial_sums, 'rep', scatter_dimension=0, tiled=True)  66 us
    psum x2, blocking collectives, _manage_run(): own_rows = lax.psum(own_rows, axis_name=w)  53.8 us
    all_gather x1, waiting for transfers between devices, per_device(): lax.all_gather(message, 'rep', axis=0, tiled=True)  33.9 us
    mul x1, local copies, waits for them, and re-layouts, per_device(): dense * keeper[:, None, :, :, None]  27.7 us
    reduce_scatter x1, waiting for transfers between devices, per_device(): lax.psum_scatter(partial_back.astype(jnp.bfloat16), 'row', scatter_dimens...  23.4 us
    mul x1, other arithmetic, per_device(): dense * keeper[:, None, :, :, None]  19.8 us
    dot_general x1, matrix products, per_device(): jnp.dot(strip, lax.all_gather(own, 'row', axis=0, tiled=True), preferred_...  12.6 us
  transfers between devices with their start and end apart: 6, of which 5 were waited for; matrix products, arithmetic and copies ran while one was open for 15% of the time, Pallas kernels for 0%

profile of v1, /device:TPU:1, one launch (start us, length us, event | category | flops | bytes accessed | tf_op | source)
XLA Modules:
  0.0 475.3 jit_solution(5848590697566996618)
XLA Ops:
  7.2 0.0 copy-start
  7.2 0.0 all-gather.3.cloned.1.call-start
  7.2 1.5 copy-done
  8.8 0.7 constant_dynamic-slice_fusion
  9.4 0.0 all-gather.3.cloned.1.call-update
  9.5 0.0 reduce-scatter.3.cloned.1.call-start
  9.5 0.8 copy.14
  10.3 0.7 broadcast_compare_fusion
  11.0 0.1 copy.15
  11.1 6.3 %convert_element_type.45 = bf16[4096,8,128]{2,1,0:T(8,128)(2,1)S(1)} convert(s32[4096,8,128]{2,1,0:T(8,128)} %param.13) | non-fusion elementwise | flops 4194304 | bytes 25165824 | tf_op jit(solution)/shard_map/convert_element_type | solution.py:45
  17.4 0.1 fusion.13
  17.5 19.8 %broadcast_multiply_fusion = bf16[32,128,8,2,128]{4,3,2,1,0:T(2,128)(2,1)} fusion(bf16[32,8,2]{2,1,0:T(8,128)(2,1)S(1)} %fusion.13, bf16[32,128,8,128]{3,2,1,0:T(8,128)(2,1)S(1)} %bitcast.15), kind=kLoop, calls=%fused_computation | loop fusion | flops 8388608 | bytes 25166848 | tf_op jit(solution)/shard_map/mul | solution.py:48
  37.3 27.7 %mul.80 = bf16[4096,2048]{1,0:T(8,128)(2,1)} reshape(bf16[32,128,8,2,128]{4,3,2,1,0:T(2,128)(2,1)} %broadcast_multiply_fusion) | data formatting | bytes 33554432 | tf_op jit(solution)/shard_map/mul | solution.py:48
  65.1 0.0 copy-start.4
  65.1 0.0 copy-start.2
  65.1 0.0 copy-start.3
  65.1 0.0 copy-start.5
  65.1 0.0 copy-start.6
  65.1 0.0 copy-start.7
  65.1 0.0 all-gather.3.cloned.1.call-done
  65.1 12.6 %fusion.17 = f32[4096,256]{1,0:T(8,128)} fusion(bf16[4096,2048]{1,0:T(8,128)(2,1)} %mul.80, bf16[2048,256]{1,0:T(8,128)(2,1)} %all-gather.3.cloned.1.call-done), kind=kOutput, calls=%fused_computation.33 | convolution fusion | flops 4294967296 | bytes 22020096 | tf_op jit(solution)/shard_map/dot_general | solution.py:51
  77.7 0.0 reduce-scatter.3.cloned.1.call-update
  77.8 0.0 all-gather.5.cloned.1.call-start
  77.8 0.0 copy-done.4
  77.8 0.0 copy-done.2
  77.9 0.0 copy-done.3
  77.9 0.2 fusion.16
  78.1 66.0 %reduce-scatter.3.cloned.1.call-done = f32[256,256]{1,0:T(8,128)} async-done(((f32[4096,256]{1,0:T(8,128)}), f32[256,256]{1,0:T(8,128)}) %reduce-scatter.3.cloned.1.call-update) | async-done | bytes 262160 | tf_op jit(solution)/shard_map/reduce_scatter | solution.py:54
  144.1 0.0 copy-done.5
  144.1 0.0 copy-done.6
  144.1 0.0 copy-done.7
  144.1 2.0 fusion.14
  146.1 0.9 fusion.2
  147.0 0.0 all-gather.5.cloned.1.call-update
  147.0 0.0 all-reduce.7.cloned.1.call-start
  147.1 0.9 convolution_multiply_fusion.1
  148.0 2.0 convolution_multiply_fusion
  150.0 0.0 all-reduce.7.cloned.1.call-update
  150.0 0.0 copy-start.1
  150.0 0.2 reduce-scatter.5.cloned.1.call-start
  150.2 33.9 %all-gather.5.cloned.1.call-done = bf16[4096,256]{1,0:T(8,128)(2,1)} async-done(((bf16[256,256]{1,0:T(8,128)(2,1)}), bf16[4096,256]{1,0:T(8,128)(2,1)}) %all-gather.5.cloned.1.call-update) | async-done | bytes 2097168 | tf_op jit(solution)/shard_map/all_gather | solution.py:85
  184.1 12.3 %convolution_convert_fusion = bf16[2048,256]{1,0:T(8,128)(2,1)} fusion(bf16[4096,2048]{1,0:T(8,128)(2,1)} %mul.80, bf16[4096,256]{1,0:T(8,128)(2,1)} %all-gather.5.cloned.1.call-done), kind=kOutput, calls=%fused_computation.1 | convolution fusion | flops 4295491584 | bytes 19922944 | tf_op jit(solution)/shard_map/dot_general | solution.py:83
  196.4 0.0 reduce-scatter.5.cloned.1.call-update
  196.4 0.0 all-reduce.5.cloned.1.call-start
  196.5 70.4 %all-reduce.7.cloned.1.call-done = (f32[256,256]{1,0:T(8,128)}, f32[256,256]{1,0:T(8,128)}) async-done(((f32[256,256]{1,0:T(8,128)}, f32[256,256]{1,0:T(8,128)}), (f32[256,256]{1,0:T(8,128)}, f32[256,256]{1,0:T(8,128)})) %all-reduce.7.cloned.1.call-update) | async-done | bytes 524304 | tf_op jit(solution)/shard_map/psum | solution.py:28
  266.9 0.0 all-reduce.5.cloned.1.call-update
  266.9 17.5 %psum.46 = f32[256]{0:T(256)S(1)} all-reduce(f32[256]{0:T(256)S(1)} %broadcast_multiply_fusion.1), channel_id=1, replica_groups=mesh['row'=8,'rep'=16] {'row'}, use_global_device_ids=true, to_apply=%region_7.0 | all-reduce | flops 256 | bytes 2048 | tf_op jit(solution)/shard_map/psum | solution.py:28
  284.4 36.2 %psum.47 = f32[256]{0:T(256)} all-reduce(f32[256]{0:T(256)S(1)} %psum.46), channel_id=1, replica_groups=mesh['row'=8,'rep'=16] {'rep'}, use_global_device_ids=true, to_apply=%region_8.0 | all-reduce | flops 256 | bytes 2048 | tf_op jit(solution)/shard_map/psum | solution.py:28
  320.7 23.4 %reduce-scatter.5.cloned.1.call-done = bf16[256,256]{1,0:T(8,128)(2,1)} async-done(((bf16[2048,256]{1,0:T(8,128)(2,1)}), bf16[256,256]{1,0:T(8,128)(2,1)}) %reduce-scatter.5.cloned.1.call-update) | async-done | bytes 131088 | tf_op jit(solution)/shard_map/reduce_scatter | solution.py:89
  344.1 1.8 fusion.1
  345.9 119.3 %all-reduce.5.cloned.1.call-done = (f32[256,256]{1,0:T(8,128)}, f32[256,256]{1,0:T(8,128)}) async-done(((f32[256,256]{1,0:T(8,128)}, f32[256,256]{1,0:T(8,128)}), (f32[256,256]{1,0:T(8,128)}, f32[256,256]{1,0:T(8,128)})) %all-reduce.5.cloned.1.call-update) | async-done | bytes 524304 | tf_op jit(solution)/shard_map/psum | solution.py:28
  465.1 1.7 copy.20
  466.8 1.7 copy.21
  468.5 0.0 copy-done.1
  (2 shorter events, 0.0 us)
Async XLA Ops:
  7.2 1.6 copy-start
  7.2 58.0 %all-gather.3.cloned.1.call-start = ((), (), s32[]{:S(2)}) async-start(), calls=%async_computation.2 | async-start | bytes 1179648 | tf_op jit(solution)/shard_map/all_gather | solution.py:52
  9.5 134.6 %reduce-scatter.3.cloned.1.call-start = ((), (), s32[]{:S(2)}) async-start(), calls=%async_computation.3 | async-start | bytes 4456448 | tf_op jit(solution)/shard_map/reduce_scatter | solution.py:54
  65.1 12.7 %copy-start.4 = (s32[256]{0:T(256)S(1)}, s32[256]{0:T(256)}, u32[]{:S(2)}) copy-start(s32[256]{0:T(256)} %param.16) | copy-start | bytes 3076
  65.1 12.8 %copy-start.2 = (bf16[256,256]{1,0:T(8,128)(2,1)S(1)}, bf16[256,256]{1,0:T(8,128)(2,1)}, u32[]{:S(2)}) copy-start(bf16[256,256]{1,0:T(8,128)(2,1)} %constant_dynamic-slice_fusion) | copy-start | bytes 393220
  65.1 12.8 %copy-start.3 = (bf16[256,256]{1,0:T(8,128)(2,1)S(1)}, bf16[256,256]{1,0:T(8,128)(2,1)}, u32[]{:S(2)}) copy-start(bf16[256,256]{1,0:T(8,128)(2,1)} %param.10) | copy-start | bytes 393220
  65.1 79.0 %copy-start.5 = (bf16[256,256]{1,0:T(8,128)(2,1)S(1)}, bf16[256,256]{1,0:T(8,128)(2,1)}, u32[]{:S(2)}) copy-start(bf16[256,256]{1,0:T(8,128)(2,1)} %param.17) | copy-start | bytes 393220
  65.1 79.0 %copy-start.6 = (bf16[256,256]{1,0:T(8,128)(2,1)S(1)}, bf16[256,256]{1,0:T(8,128)(2,1)}, u32[]{:S(2)}) copy-start(bf16[256,256]{1,0:T(8,128)(2,1)} %param.11) | copy-start | bytes 393220
  65.1 79.0 %copy-start.7 = (f32[256]{0:T(256)S(1)}, f32[256]{0:T(256)}, u32[]{:S(2)}) copy-start(f32[256]{0:T(256)} %param.12) | copy-start | bytes 3076
  77.8 106.3 %all-gather.5.cloned.1.call-start = ((), (), s32[]{:S(2)}) async-start(), calls=%async_computation.4 | async-start | bytes 2228224 | tf_op jit(solution)/shard_map/all_gather | solution.py:85
  147.0 119.8 %all-reduce.7.cloned.1.call-start = ((), (), s32[]{:S(2)}) async-start(), calls=%async_computation.7 | async-start | bytes 1048576 | tf_op jit(solution)/shard_map/psum | solution.py:28
  150.0 318.5 %copy-start.1 = (bf16[4096,256]{1,0:T(8,128)(2,1)S(1)}, bf16[4096,256]{1,0:T(8,128)(2,1)}, u32[]{:S(2)}) copy-start(bf16[4096,256]{1,0:T(8,128)(2,1)} %param.9) | copy-start | bytes 6291460
  150.0 194.1 %reduce-scatter.5.cloned.1.call-start = ((), (), s32[]{:S(2)}) async-start(), calls=%async_computation.5 | async-start | bytes 1179648 | tf_op jit(solution)/shard_map/reduce_scatter | solution.py:89
  196.4 268.7 %all-reduce.5.cloned.1.call-start = ((), (), s32[]{:S(2)}) async-start(), calls=%async_computation.6 | async-start | bytes 1048576 | tf_op jit(solution)/shard_map/psum | solution.py:28
Sparse Core Ops, SparseCore 0:
  11.0 48.4 all-gather.2
  77.9 66.1 reduce-scatter.2
  147.1 36.9 all-gather.4
  187.1 79.7 all-reduce.6
  270.7 73.2 reduce-scatter.4
  346.4 118.6 all-reduce.4
